TPU v7x, 32 devices: a whole 2x2x4 slice. The times are simulated.
32 devices in a mesh: pair: 8 (over y, x, core), ints: 4 (over z).
Axes of the slice: x: 2, y: 2, z: 4, core: 2. Of those that a mesh axis runs over, the one named last changes fastest.
Arguments:
- t_amps: bfloat16 [32, 8, 4096], P('pair', None, 'ints'), may hold values from -6 to 6
- block_mask: int32 [32, 8, 64], P('pair', None, 'ints'), may hold values 0 or 1
- factors: bfloat16 [8, 64, 64, 128], P('pair', 'ints'), may hold values from -0.75 to 0.75
- links: int32 [8, 64, 32], P('pair', 'ints'), may hold values from 0 to 63, as said below
- link_counts: int32 [8, 64], P('pair', 'ints'), may hold values from 8 to 32, as said below
Outputs:
- ladder: bfloat16 [32, 8, 4096], P('pair', None, 'ints')
Inputs may be any that keep to these rules, and one draw needn't show every extreme that they name: `links`: the 32 slots of a tile name distinct tiles of its own block; only the first link_counts slots are used. `link_counts`: in every block, tile 0 uses all 32 slots.
All inputs are finite; a program needn't handle non-finite values. No bound on the sum of `block_mask` on one device may be relied on, other than what follows from the above.
Results may differ from a plain program's by a relative error of at most 0.008.
Values may be sent and summed in bfloat16 or wider, within the bound.
A program may use at most 128 MiB of HBM per device.

v0:
```python
import jax
import jax.numpy as jnp
from jax import lax
from jax.sharding import PartitionSpec as P


def split_high(values):
    high = values.astype(jnp.bfloat16)
    rest = (values - high.astype(jnp.float32)).astype(jnp.bfloat16)
    return (high, rest)


def tile_ladder(all_f, all_t, own_f, link_rows, count_rows):
    slots = jnp.arange(link_rows.shape[-1], dtype=jnp.int32)
    npairs = all_t.shape[0]
    tile = own_f.shape[1]
    amp_tiles = all_t.reshape(npairs, all_f.shape[0], tile)

    def one_tile(inputs):
        own, index_row, count = inputs
        near_f = jnp.take(all_f, index_row, axis=0)
        near_t = jnp.take(amp_tiles, index_row, axis=1)
        used = (slots < count).astype(jnp.float32)
        blocks = jnp.einsum("xq,kyq->kxy", own, near_f, preferred_element_type=jnp.float32)
        blocks = blocks * used[:, None, None]
        high, rest = split_high(blocks)
        first = jnp.einsum("kxy,pky->px", high, near_t, preferred_element_type=jnp.float32)
        second = jnp.einsum("kxy,pky->px", rest, near_t, preferred_element_type=jnp.float32)
        return first + second

    stacked = lax.map(one_tile, (own_f, link_rows, count_rows))
    return jnp.transpose(stacked, (1, 0, 2)).reshape(npairs, own_f.shape[0] * tile)


def body(t_amps, block_mask, factors, links, link_counts):
    own_f = factors[0]
    link_rows = links[0]
    count_rows = link_counts[0]
    tile_count = own_f.shape[0]
    tile = own_f.shape[1]
    pair_dev, nblocks, width = t_amps.shape
    shaped = t_amps.reshape(pair_dev, nblocks, tile_count, tile)
    masked = (shaped * block_mask[:, :, :, None].astype(t_amps.dtype)).reshape(
        pair_dev, nblocks, width
    )
    local = lax.all_to_all(masked, "pair", split_axis=1, concat_axis=0, tiled=True)[:, 0, :]
    all_f, all_t = (
        lax.all_gather(own_f, "ints", axis=0, tiled=True),
        lax.all_gather(local, "ints", axis=1, tiled=True),
    )
    result = tile_ladder(all_f, all_t, own_f, link_rows, count_rows)
    rounded = result.astype(jnp.bfloat16)[:, None, :]
    return lax.all_to_all(rounded, "pair", split_axis=0, concat_axis=1, tiled=True)


def solution(mesh):
    placed = (
        P("pair", None, "ints"),
        P("pair", None, "ints"),
        P("pair", "ints", None, None),
        P("pair", "ints", None),
        P("pair", "ints"),
    )
    return jax.shard_map(
        body, mesh=mesh, in_specs=placed, out_specs=P("pair", None, "ints"), check_vma=False
    )
```

profile of v0, /device:TPU:0, one launch (start us, length us, event | category | flops | bytes accessed | tf_op | source)
XLA Modules:
  0.0 173.8 jit_solution(7210912905600619136)
XLA Ops:
  9.0 5.2 %all-to-all-start = ((bf16[4,8,1024]{2,0,1:T(4,128)(2,1)}), bf16[4,8,1024]{2,0,1:T(4,128)(2,1)S(1)}, u32[]{:S(2)}, u32[]{:S(2)}) async-start(bf16[4,8,1024]{2,0,1:T(4,128)(2,1)} %copy.27), calls=%async_computation | async-start | bytes 131072 | tf_op jit(solution)/shard_map/all_to_all | solution.py:46
  14.2 5.0 %all-to-all-done = bf16[4,8,1024]{2,0,1:T(4,128)(2,1)S(1)} async-done(((bf16[4,8,1024]{2,0,1:T(4,128)(2,1)}), bf16[4,8,1024]{2,0,1:T(4,128)(2,1)S(1)}, u32[]{:S(2)}, u32[]{:S(2)}) %all-to-all-start) | async-done | bytes 65568 | tf_op jit(solution)/shard_map/all_to_all | solution.py:46
  19.2 16.7 %all_gather.6 = bf16[32,4096]{1,0:T(8,128)(2,1)S(1)} all-gather(bf16[32,1024]{1,0:T(8,128)(2,1)S(1)} %squeeze.27), channel_id=1, replica_groups=mesh['pair'=8,'ints'=4] {'ints'}, dimensions={1}, use_global_device_ids=true | all-gather | bytes 327680 | tf_op jit(solution)/shard_map/all_gather | solution.py:49
  36.8 7.0 %all-gather.3.cloned.1.call-done = bf16[1,64,64,128]{3,2,0,1:T(8,128)(2,1)} async-done(((bf16[1,16,64,128]{3,2,0,1:T(8,128)(2,1)}), bf16[1,64,64,128]{3,2,0,1:T(8,128)(2,1)}) %all-gather.3.cloned.1.call-update) | async-done | bytes 1048592 | tf_op jit(solution)/shard_map/all_gather | solution.py:48
  44.5 110.9 %while.11 = (s32[]{:T(128)}, bf16[16,32,64]{2,1,0:T(8,128)(2,1)S(1)}, s32[16,32]{1,0:T(8,128)}, bf16[32,64,64]{2,0,1:T(8,128)(2,1)S(1)}, bf16[64,64,128]{2,1,0:T...) while((s32[]{:T(128)}, bf16[16,32,64]{2,1,0:T(8,128)(2,1)S(1)}, ...), condition=%wide.region_1.2_spmd.clone, body=%wide.region_0.1_spmd.clone.sunk | while | flops 51514720 | bytes 4389073 | solution.py:31
  45.1 1.3 compare_convert_fusion.2
  47.1 1.9 %gather_fusion = bf16[32,64,128]{2,1,0:T(8,128)(2,1)S(1)} fusion(bf16[64,64,128]{2,1,0:T(8,128)(2,1)} %get-tuple-element.168, s32[1024]{0:T(1024)S(1)} %pad_clamp_fusion.2), kind=kCustom, calls=%fused_computation.1.clone.clone.1 | custom fusion | bytes 1048704 | tf_op jit(solution)/shard_map/while/body/eval_jaxpr/jit(_take)/gather | solution.py:21
  52.0 1.3 compare_convert_fusion.2
  54.1 1.9 %gather_fusion = bf16[32,64,128]{2,1,0:T(8,128)(2,1)S(1)} fusion(bf16[64,64,128]{2,1,0:T(8,128)(2,1)} %get-tuple-element.168, s32[1024]{0:T(1024)S(1)} %pad_clamp_fusion.2), kind=kCustom, calls=%fused_computation.1.clone.clone.1 | custom fusion | bytes 1048704 | tf_op jit(solution)/shard_map/while/body/eval_jaxpr/jit(_take)/gather | solution.py:21
  61.0 1.9 %gather_fusion = bf16[32,64,128]{2,1,0:T(8,128)(2,1)S(1)} fusion(bf16[64,64,128]{2,1,0:T(8,128)(2,1)} %get-tuple-element.168, s32[1024]{0:T(1024)S(1)} %pad_clamp_fusion.2), kind=kCustom, calls=%fused_computation.1.clone.clone.1 | custom fusion | bytes 1048704 | tf_op jit(solution)/shard_map/while/body/eval_jaxpr/jit(_take)/gather | solution.py:21
  67.9 1.9 %gather_fusion = bf16[32,64,128]{2,1,0:T(8,128)(2,1)S(1)} fusion(bf16[64,64,128]{2,1,0:T(8,128)(2,1)} %get-tuple-element.168, s32[1024]{0:T(1024)S(1)} %pad_clamp_fusion.2), kind=kCustom, calls=%fused_computation.1.clone.clone.1 | custom fusion | bytes 1048704 | tf_op jit(solution)/shard_map/while/body/eval_jaxpr/jit(_take)/gather | solution.py:21
  74.9 1.9 %gather_fusion = bf16[32,64,128]{2,1,0:T(8,128)(2,1)S(1)} fusion(bf16[64,64,128]{2,1,0:T(8,128)(2,1)} %get-tuple-element.168, s32[1024]{0:T(1024)S(1)} %pad_clamp_fusion.2), kind=kCustom, calls=%fused_computation.1.clone.clone.1 | custom fusion | bytes 1048704 | tf_op jit(solution)/shard_map/while/body/eval_jaxpr/jit(_take)/gather | solution.py:21
  81.8 1.9 %gather_fusion = bf16[32,64,128]{2,1,0:T(8,128)(2,1)S(1)} fusion(bf16[64,64,128]{2,1,0:T(8,128)(2,1)} %get-tuple-element.168, s32[1024]{0:T(1024)S(1)} %pad_clamp_fusion.2), kind=kCustom, calls=%fused_computation.1.clone.clone.1 | custom fusion | bytes 1048704 | tf_op jit(solution)/shard_map/while/body/eval_jaxpr/jit(_take)/gather | solution.py:21
  88.7 1.9 %gather_fusion = bf16[32,64,128]{2,1,0:T(8,128)(2,1)S(1)} fusion(bf16[64,64,128]{2,1,0:T(8,128)(2,1)} %get-tuple-element.168, s32[1024]{0:T(1024)S(1)} %pad_clamp_fusion.2), kind=kCustom, calls=%fused_computation.1.clone.clone.1 | custom fusion | bytes 1048704 | tf_op jit(solution)/shard_map/while/body/eval_jaxpr/jit(_take)/gather | solution.py:21
  95.6 1.9 %gather_fusion = bf16[32,64,128]{2,1,0:T(8,128)(2,1)S(1)} fusion(bf16[64,64,128]{2,1,0:T(8,128)(2,1)} %get-tuple-element.168, s32[1024]{0:T(1024)S(1)} %pad_clamp_fusion.2), kind=kCustom, calls=%fused_computation.1.clone.clone.1 | custom fusion | bytes 1048704 | tf_op jit(solution)/shard_map/while/body/eval_jaxpr/jit(_take)/gather | solution.py:21
  102.6 1.9 %gather_fusion = bf16[32,64,128]{2,1,0:T(8,128)(2,1)S(1)} fusion(bf16[64,64,128]{2,1,0:T(8,128)(2,1)} %get-tuple-element.168, s32[1024]{0:T(1024)S(1)} %pad_clamp_fusion.2), kind=kCustom, calls=%fused_computation.1.clone.clone.1 | custom fusion | bytes 1048704 | tf_op jit(solution)/shard_map/while/body/eval_jaxpr/jit(_take)/gather | solution.py:21
  109.5 1.9 %gather_fusion = bf16[32,64,128]{2,1,0:T(8,128)(2,1)S(1)} fusion(bf16[64,64,128]{2,1,0:T(8,128)(2,1)} %get-tuple-element.168, s32[1024]{0:T(1024)S(1)} %pad_clamp_fusion.2), kind=kCustom, calls=%fused_computation.1.clone.clone.1 | custom fusion | bytes 1048704 | tf_op jit(solution)/shard_map/while/body/eval_jaxpr/jit(_take)/gather | solution.py:21
  116.4 1.9 %gather_fusion = bf16[32,64,128]{2,1,0:T(8,128)(2,1)S(1)} fusion(bf16[64,64,128]{2,1,0:T(8,128)(2,1)} %get-tuple-element.168, s32[1024]{0:T(1024)S(1)} %pad_clamp_fusion.2), kind=kCustom, calls=%fused_computation.1.clone.clone.1 | custom fusion | bytes 1048704 | tf_op jit(solution)/shard_map/while/body/eval_jaxpr/jit(_take)/gather | solution.py:21
  123.4 1.9 %gather_fusion = bf16[32,64,128]{2,1,0:T(8,128)(2,1)S(1)} fusion(bf16[64,64,128]{2,1,0:T(8,128)(2,1)} %get-tuple-element.168, s32[1024]{0:T(1024)S(1)} %pad_clamp_fusion.2), kind=kCustom, calls=%fused_computation.1.clone.clone.1 | custom fusion | bytes 1048704 | tf_op jit(solution)/shard_map/while/body/eval_jaxpr/jit(_take)/gather | solution.py:21
  130.3 1.9 %gather_fusion = bf16[32,64,128]{2,1,0:T(8,128)(2,1)S(1)} fusion(bf16[64,64,128]{2,1,0:T(8,128)(2,1)} %get-tuple-element.168, s32[1024]{0:T(1024)S(1)} %pad_clamp_fusion.2), kind=kCustom, calls=%fused_computation.1.clone.clone.1 | custom fusion | bytes 1048704 | tf_op jit(solution)/shard_map/while/body/eval_jaxpr/jit(_take)/gather | solution.py:21
  137.2 1.9 %gather_fusion = bf16[32,64,128]{2,1,0:T(8,128)(2,1)S(1)} fusion(bf16[64,64,128]{2,1,0:T(8,128)(2,1)} %get-tuple-element.168, s32[1024]{0:T(1024)S(1)} %pad_clamp_fusion.2), kind=kCustom, calls=%fused_computation.1.clone.clone.1 | custom fusion | bytes 1048704 | tf_op jit(solution)/shard_map/while/body/eval_jaxpr/jit(_take)/gather | solution.py:21
  144.2 1.9 %gather_fusion = bf16[32,64,128]{2,1,0:T(8,128)(2,1)S(1)} fusion(bf16[64,64,128]{2,1,0:T(8,128)(2,1)} %get-tuple-element.168, s32[1024]{0:T(1024)S(1)} %pad_clamp_fusion.2), kind=kCustom, calls=%fused_computation.1.clone.clone.1 | custom fusion | bytes 1048704 | tf_op jit(solution)/shard_map/while/body/eval_jaxpr/jit(_take)/gather | solution.py:21
  151.1 1.9 %gather_fusion = bf16[32,64,128]{2,1,0:T(8,128)(2,1)S(1)} fusion(bf16[64,64,128]{2,1,0:T(8,128)(2,1)} %get-tuple-element.168, s32[1024]{0:T(1024)S(1)} %pad_clamp_fusion.2), kind=kCustom, calls=%fused_computation.1.clone.clone.1 | custom fusion | bytes 1048704 | tf_op jit(solution)/shard_map/while/body/eval_jaxpr/jit(_take)/gather | solution.py:21
  157.1 8.7 %all_to_all.33 = bf16[8,2,2048]{2,1,0:T(2,128)(2,1)S(1)} all-to-all(bf16[8,2,2048]{2,1,0:T(2,128)(2,1)S(1)} %reshape.86), channel_id=1, replica_groups=mesh['pair'=8,'ints'=4] {'pair'}, dimensions={0} | all-to-all | bytes 131072 | tf_op jit(solution)/shard_map/all_to_all | solution.py:53
  (152 shorter events, 84.2 us)
Async XLA Ops:
  6.5 37.3 %all-gather.3.cloned.1.call-start = ((), (), s32[]{:S(2)}) async-start(), calls=%async_computation.2 | async-start | bytes 1310720 | tf_op jit(solution)/shard_map/all_gather | solution.py:48
  6.5 0.7 copy-start.1
  7.4 0.8 copy-start
  9.0 10.2 %all-to-all-start = ((bf16[4,8,1024]{2,0,1:T(4,128)(2,1)}), bf16[4,8,1024]{2,0,1:T(4,128)(2,1)S(1)}, u32[]{:S(2)}, u32[]{:S(2)}) async-start(bf16[4,8,1024]{2,0,1:T(4,128)(2,1)} %copy.27), calls=%async_computation | async-start | bytes 131072 | tf_op jit(solution)/shard_map/all_to_all | solution.py:46
  43.9 0.7 copy-start.2
Sparse Core Ops, SparseCore 0:
  8.9 34.9 all-gather.2
where the time goes:
time: 177 us; the launch traced here: 174 us
  local copies, waits for them, and re-layouts  53.6 us (30%)
  other arithmetic  34.1 us (19%)
  matrix products  28.4 us (16%)
  blocking collectives  25.4 us (14%)
  between operations  13.5 us (8%)
  waiting for transfers between devices  12.7 us (7%)
  starting transfers between devices  5.2 us (3%)
    gather x16, local copies, waits for them, and re-layouts, one_tile(): near_f = jnp.take(all_f, index_row, axis=0)  29.9 us
    convert_element_type x16, other arithmetic, one_tile(): used = (slots < count).astype(jnp.float32)  21.5 us
    dot_general x16, matrix products, one_tile(): jnp.einsum('xq,kyq->kxy', own, near_f, preferred_element_type=jnp.float32)  17.1 us
    all_gather x1, blocking collectives, body(): lax.all_gather(local, 'ints', axis=1, tiled=True)  16.7 us
    select_n x16, other arithmetic, one_tile(): near_t = jnp.take(amp_tiles, index_row, axis=1)  11.1 us
    gather x16, local copies, waits for them, and re-layouts, one_tile(): near_t = jnp.take(amp_tiles, index_row, axis=1)  9.63 us
    dynamic_slice x16, local copies, waits for them, and re-layouts, tile_ladder(): stacked = lax.map(one_tile, (own_f, link_rows, count_rows))  9.38 us
    all_to_all x1, blocking collectives, body(): lax.all_to_all(rounded, 'pair', split_axis=0, concat_axis=1, tiled=True)  8.66 us
  transfers between devices with their start and end apart: 2, of which 2 were waited for; matrix products, arithmetic and copies ran while one was open for 1% of the time, Pallas kernels for 0%

commit v1 on v0

--- a/solution.py
+++ b/solution.py
@@ -2,6 +2,16 @@
 import jax.numpy as jnp
 from jax import lax
 from jax.sharding import PartitionSpec as P
+
+
+def ring_gather(x, axis, dim):
+    ways, here, step = (lax.axis_size(axis), lax.axis_index(axis), x.shape[dim])
+    dims = [n * ways if d == dim else n for d, n in enumerate(x.shape)]
+    full = lax.dynamic_update_slice_in_dim(jnp.zeros(dims, x.dtype), x, here * step, axis=dim)
+    for far in range(1, ways):
+        x = lax.ppermute(x, axis, [(d, (d + 1) % ways) for d in range(ways)])
+        full = lax.dynamic_update_slice_in_dim(full, x, (here - far) % ways * step, axis=dim)
+    return full
 
 
 def split_high(values):
@@ -46,7 +56,7 @@
     local = lax.all_to_all(masked, "pair", split_axis=1, concat_axis=0, tiled=True)[:, 0, :]
     all_f, all_t = (
         lax.all_gather(own_f, "ints", axis=0, tiled=True),
-        lax.all_gather(local, "ints", axis=1, tiled=True),
+        ring_gather(local, "ints", 1),
     )
     result = tile_ladder(all_f, all_t, own_f, link_rows, count_rows)
     rounded = result.astype(jnp.bfloat16)[:, None, :]

time: 177 us -> 176 us (level)
  blocking collectives: 25.4 us -> 7.69 us
  waiting for transfers between devices: 12.7 us -> 27.3 us
  starting transfers between devices: 5.2 us -> 7.74 us
    ppermute x0 -> x3, waiting for transfers between devices: none -> 19.9 us  [ring_gather(): x = lax.ppermute(x, axis, [(d, (d + 1) % ways) for d in range(ways)])]
    all_gather x1 -> x0, blocking collectives: 16.7 us -> none  [body(): lax.all_gather(local, 'ints', axis=1, tiled=True)]
    all_gather x1, waiting for transfers between devices: 7.02 us -> 1.66 us  [body(): lax.all_gather(own_f, 'ints', axis=0, tiled=True)]
    ppermute x0 -> x3, starting transfers between devices: none -> 2.54 us  [ring_gather(): x = lax.ppermute(x, axis, [(d, (d + 1) % ways) for d in range(ways)])]
  transfers between devices with their start and end apart: 2 -> 5, of which waited for: 2 -> 5; matrix products, arithmetic and copies ran while one was open for 1% -> 1% of each run, Pallas kernels for 0% -> 0%
where the time goes in v1:
time: 176 us; the launch traced here: 173 us
  local copies, waits for them, and re-layouts  53.7 us (31%)
  other arithmetic  34.1 us (19%)
  matrix products  28.4 us (16%)
  waiting for transfers between devices  27.3 us (16%)
  between operations  13.5 us (8%)
  starting transfers between devices  7.74 us (4%)
  blocking collectives  7.69 us (4%)
    gather x16, local copies, waits for them, and re-layouts, one_tile(): near_f = jnp.take(all_f, index_row, axis=0)  29.9 us
    convert_element_type x16, other arithmetic, one_tile(): used = (slots < count).astype(jnp.float32)  21.5 us
    ppermute x3, waiting for transfers between devices, ring_gather(): x = lax.ppermute(x, axis, [(d, (d + 1) % ways) for d in range(ways)])  19.9 us
    dot_general x16, matrix products, one_tile(): jnp.einsum('xq,kyq->kxy', own, near_f, preferred_element_type=jnp.float32)  17.1 us
    select_n x16, other arithmetic, one_tile(): near_t = jnp.take(amp_tiles, index_row, axis=1)  11.1 us
    gather x16, local copies, waits for them, and re-layouts, one_tile(): near_t = jnp.take(amp_tiles, index_row, axis=1)  9.63 us
    dynamic_slice x16, local copies, waits for them, and re-layouts, tile_ladder(): stacked = lax.map(one_tile, (own_f, link_rows, count_rows))  9.38 us
    all_to_all x1, blocking collectives, body(): lax.all_to_all(rounded, 'pair', split_axis=0, concat_axis=1, tiled=True)  7.69 us
  transfers between devices with their start and end apart: 5, of which 5 were waited for; matrix products, arithmetic and copies ran while one was open for 1% of the time, Pallas kernels for 0%

profile of v1, /device:TPU:0, one launch (start us, length us, event | category | flops | bytes accessed | tf_op | source)
XLA Modules:
  0.0 173.2 jit_solution(7790041238544437167)
XLA Ops:
  9.0 5.2 %all-to-all-start = ((bf16[4,8,1024]{2,0,1:T(4,128)(2,1)}), bf16[4,8,1024]{2,0,1:T(4,128)(2,1)S(1)}, u32[]{:S(2)}, u32[]{:S(2)}) async-start(bf16[4,8,1024]{2,0,1:T(4,128)(2,1)} %copy.32), calls=%async_computation | async-start | bytes 131072 | tf_op jit(solution)/shard_map/all_to_all | solution.py:56
  14.2 5.0 %all-to-all-done = bf16[4,8,1024]{2,0,1:T(4,128)(2,1)S(1)} async-done(((bf16[4,8,1024]{2,0,1:T(4,128)(2,1)}), bf16[4,8,1024]{2,0,1:T(4,128)(2,1)S(1)}, u32[]{:S(2)}, u32[]{:S(2)}) %all-to-all-start) | async-done | bytes 65568 | tf_op jit(solution)/shard_map/all_to_all | solution.py:56
  20.9 5.7 %collective-permute-done = bf16[32,1024]{1,0:T(8,128)(2,1)S(1)} collective-permute-done((bf16[32,1024]{1,0:T(8,128)(2,1)S(1)}, bf16[32,1024]{1,0:T(8,128)(2,1)S(1)}, u32[]{:S(2)}, u32[]{:S(2)}) %collective-permute-start) | collective-permute-done | bytes 65568 | tf_op jit(solution)/shard_map/ppermute | solution.py:12
  26.8 7.3 %collective-permute-done.1 = bf16[32,1024]{1,0:T(8,128)(2,1)S(1)} collective-permute-done((bf16[32,1024]{1,0:T(8,128)(2,1)S(1)}, bf16[32,1024]{1,0:T(8,128)(2,1)S(1)}, u32[]{:S(2)}, u32[]{:S(2)}) %collective-permute-start.1) | collective-permute-done | bytes 65568 | tf_op jit(solution)/shard_map/ppermute | solution.py:12
  34.9 6.9 %collective-permute-done.2 = bf16[32,1024]{1,0:T(8,128)(2,1)S(1)} collective-permute-done((bf16[32,1024]{1,0:T(8,128)(2,1)S(1)}, bf16[32,1024]{1,0:T(8,128)(2,1)S(1)}, u32[]{:S(2)}, u32[]{:S(2)}) %collective-permute-start.2) | collective-permute-done | bytes 65568 | tf_op jit(solution)/shard_map/ppermute | solution.py:12
  42.6 1.7 all-gather.3.cloned.1.call-done
  45.0 110.9 %while.11 = (s32[]{:T(128)}, bf16[16,32,64]{2,1,0:T(8,128)(2,1)S(1)}, s32[16,32]{1,0:T(8,128)}, bf16[32,64,64]{2,0,1:T(8,128)(2,1)S(1)}, bf16[64,64,128]{2,1,0:T...) while((s32[]{:T(128)}, bf16[16,32,64]{2,1,0:T(8,128)(2,1)S(1)}, ...), condition=%wide.region_1.2_spmd.clone, body=%wide.region_0.1_spmd.clone.sunk | while | flops 51514720 | bytes 4389073 | solution.py:41
  47.6 1.9 %gather_fusion = bf16[32,64,128]{2,1,0:T(8,128)(2,1)S(1)} fusion(bf16[64,64,128]{2,1,0:T(8,128)(2,1)} %get-tuple-element.168, s32[1024]{0:T(1024)S(1)} %pad_clamp_fusion.2), kind=kCustom, calls=%fused_computation.1.clone.clone.1 | custom fusion | bytes 1048704 | tf_op jit(solution)/shard_map/while/body/eval_jaxpr/jit(_take)/gather | solution.py:31
  54.5 1.9 %gather_fusion = bf16[32,64,128]{2,1,0:T(8,128)(2,1)S(1)} fusion(bf16[64,64,128]{2,1,0:T(8,128)(2,1)} %get-tuple-element.168, s32[1024]{0:T(1024)S(1)} %pad_clamp_fusion.2), kind=kCustom, calls=%fused_computation.1.clone.clone.1 | custom fusion | bytes 1048704 | tf_op jit(solution)/shard_map/while/body/eval_jaxpr/jit(_take)/gather | solution.py:31
  61.4 1.9 %gather_fusion = bf16[32,64,128]{2,1,0:T(8,128)(2,1)S(1)} fusion(bf16[64,64,128]{2,1,0:T(8,128)(2,1)} %get-tuple-element.168, s32[1024]{0:T(1024)S(1)} %pad_clamp_fusion.2), kind=kCustom, calls=%fused_computation.1.clone.clone.1 | custom fusion | bytes 1048704 | tf_op jit(solution)/shard_map/while/body/eval_jaxpr/jit(_take)/gather | solution.py:31
  68.4 1.9 %gather_fusion = bf16[32,64,128]{2,1,0:T(8,128)(2,1)S(1)} fusion(bf16[64,64,128]{2,1,0:T(8,128)(2,1)} %get-tuple-element.168, s32[1024]{0:T(1024)S(1)} %pad_clamp_fusion.2), kind=kCustom, calls=%fused_computation.1.clone.clone.1 | custom fusion | bytes 1048704 | tf_op jit(solution)/shard_map/while/body/eval_jaxpr/jit(_take)/gather | solution.py:31
  75.3 1.9 %gather_fusion = bf16[32,64,128]{2,1,0:T(8,128)(2,1)S(1)} fusion(bf16[64,64,128]{2,1,0:T(8,128)(2,1)} %get-tuple-element.168, s32[1024]{0:T(1024)S(1)} %pad_clamp_fusion.2), kind=kCustom, calls=%fused_computation.1.clone.clone.1 | custom fusion | bytes 1048704 | tf_op jit(solution)/shard_map/while/body/eval_jaxpr/jit(_take)/gather | solution.py:31
  82.2 1.9 %gather_fusion = bf16[32,64,128]{2,1,0:T(8,128)(2,1)S(1)} fusion(bf16[64,64,128]{2,1,0:T(8,128)(2,1)} %get-tuple-element.168, s32[1024]{0:T(1024)S(1)} %pad_clamp_fusion.2), kind=kCustom, calls=%fused_computation.1.clone.clone.1 | custom fusion | bytes 1048704 | tf_op jit(solution)/shard_map/while/body/eval_jaxpr/jit(_take)/gather | solution.py:31
  89.2 1.9 %gather_fusion = bf16[32,64,128]{2,1,0:T(8,128)(2,1)S(1)} fusion(bf16[64,64,128]{2,1,0:T(8,128)(2,1)} %get-tuple-element.168, s32[1024]{0:T(1024)S(1)} %pad_clamp_fusion.2), kind=kCustom, calls=%fused_computation.1.clone.clone.1 | custom fusion | bytes 1048704 | tf_op jit(solution)/shard_map/while/body/eval_jaxpr/jit(_take)/gather | solution.py:31
  96.1 1.9 %gather_fusion = bf16[32,64,128]{2,1,0:T(8,128)(2,1)S(1)} fusion(bf16[64,64,128]{2,1,0:T(8,128)(2,1)} %get-tuple-element.168, s32[1024]{0:T(1024)S(1)} %pad_clamp_fusion.2), kind=kCustom, calls=%fused_computation.1.clone.clone.1 | custom fusion | bytes 1048704 | tf_op jit(solution)/shard_map/while/body/eval_jaxpr/jit(_take)/gather | solution.py:31
  103.0 1.9 %gather_fusion = bf16[32,64,128]{2,1,0:T(8,128)(2,1)S(1)} fusion(bf16[64,64,128]{2,1,0:T(8,128)(2,1)} %get-tuple-element.168, s32[1024]{0:T(1024)S(1)} %pad_clamp_fusion.2), kind=kCustom, calls=%fused_computation.1.clone.clone.1 | custom fusion | bytes 1048704 | tf_op jit(solution)/shard_map/while/body/eval_jaxpr/jit(_take)/gather | solution.py:31
  110.0 1.9 %gather_fusion = bf16[32,64,128]{2,1,0:T(8,128)(2,1)S(1)} fusion(bf16[64,64,128]{2,1,0:T(8,128)(2,1)} %get-tuple-element.168, s32[1024]{0:T(1024)S(1)} %pad_clamp_fusion.2), kind=kCustom, calls=%fused_computation.1.clone.clone.1 | custom fusion | bytes 1048704 | tf_op jit(solution)/shard_map/while/body/eval_jaxpr/jit(_take)/gather | solution.py:31
  116.9 1.9 %gather_fusion = bf16[32,64,128]{2,1,0:T(8,128)(2,1)S(1)} fusion(bf16[64,64,128]{2,1,0:T(8,128)(2,1)} %get-tuple-element.168, s32[1024]{0:T(1024)S(1)} %pad_clamp_fusion.2), kind=kCustom, calls=%fused_computation.1.clone.clone.1 | custom fusion | bytes 1048704 | tf_op jit(solution)/shard_map/while/body/eval_jaxpr/jit(_take)/gather | solution.py:31
  123.8 1.9 %gather_fusion = bf16[32,64,128]{2,1,0:T(8,128)(2,1)S(1)} fusion(bf16[64,64,128]{2,1,0:T(8,128)(2,1)} %get-tuple-element.168, s32[1024]{0:T(1024)S(1)} %pad_clamp_fusion.2), kind=kCustom, calls=%fused_computation.1.clone.clone.1 | custom fusion | bytes 1048704 | tf_op jit(solution)/shard_map/while/body/eval_jaxpr/jit(_take)/gather | solution.py:31
  130.7 1.9 %gather_fusion = bf16[32,64,128]{2,1,0:T(8,128)(2,1)S(1)} fusion(bf16[64,64,128]{2,1,0:T(8,128)(2,1)} %get-tuple-element.168, s32[1024]{0:T(1024)S(1)} %pad_clamp_fusion.2), kind=kCustom, calls=%fused_computation.1.clone.clone.1 | custom fusion | bytes 1048704 | tf_op jit(solution)/shard_map/while/body/eval_jaxpr/jit(_take)/gather | solution.py:31
  137.7 1.9 %gather_fusion = bf16[32,64,128]{2,1,0:T(8,128)(2,1)S(1)} fusion(bf16[64,64,128]{2,1,0:T(8,128)(2,1)} %get-tuple-element.168, s32[1024]{0:T(1024)S(1)} %pad_clamp_fusion.2), kind=kCustom, calls=%fused_computation.1.clone.clone.1 | custom fusion | bytes 1048704 | tf_op jit(solution)/shard_map/while/body/eval_jaxpr/jit(_take)/gather | solution.py:31
  144.6 1.9 %gather_fusion = bf16[32,64,128]{2,1,0:T(8,128)(2,1)S(1)} fusion(bf16[64,64,128]{2,1,0:T(8,128)(2,1)} %get-tuple-element.168, s32[1024]{0:T(1024)S(1)} %pad_clamp_fusion.2), kind=kCustom, calls=%fused_computation.1.clone.clone.1 | custom fusion | bytes 1048704 | tf_op jit(solution)/shard_map/while/body/eval_jaxpr/jit(_take)/gather | solution.py:31
  151.5 1.9 %gather_fusion = bf16[32,64,128]{2,1,0:T(8,128)(2,1)S(1)} fusion(bf16[64,64,128]{2,1,0:T(8,128)(2,1)} %get-tuple-element.168, s32[1024]{0:T(1024)S(1)} %pad_clamp_fusion.2), kind=kCustom, calls=%fused_computation.1.clone.clone.1 | custom fusion | bytes 1048704 | tf_op jit(solution)/shard_map/while/body/eval_jaxpr/jit(_take)/gather | solution.py:31
  157.6 7.7 %all_to_all.33 = bf16[8,2,2048]{2,1,0:T(2,128)(2,1)S(1)} all-to-all(bf16[8,2,2048]{2,1,0:T(2,128)(2,1)S(1)} %reshape.86), channel_id=1, replica_groups=mesh['pair'=8,'ints'=4] {'pair'}, dimensions={0} | all-to-all | bytes 131072 | tf_op jit(solution)/shard_map/all_to_all | solution.py:63
  (162 shorter events, 89.5 us)
Async XLA Ops:
  6.5 37.8 %all-gather.3.cloned.1.call-start = ((), (), s32[]{:S(2)}) async-start(), calls=%async_computation.2 | async-start | bytes 1310720 | tf_op jit(solution)/shard_map/all_gather | solution.py:58
  6.5 0.7 copy-start.1
  7.4 0.8 copy-start
  9.0 10.2 %all-to-all-start = ((bf16[4,8,1024]{2,0,1:T(4,128)(2,1)}), bf16[4,8,1024]{2,0,1:T(4,128)(2,1)S(1)}, u32[]{:S(2)}, u32[]{:S(2)}) async-start(bf16[4,8,1024]{2,0,1:T(4,128)(2,1)} %copy.32), calls=%async_computation | async-start | bytes 131072 | tf_op jit(solution)/shard_map/all_to_all | solution.py:56
  19.2 7.4 %collective-permute-start = (bf16[32,1024]{1,0:T(8,128)(2,1)S(1)}, bf16[32,1024]{1,0:T(8,128)(2,1)S(1)}, u32[]{:S(2)}, u32[]{:S(2)}) collective-permute-start(bf16[32,1024]{1,0:T(8,128)(2,1)S(1)} %squeeze.27), channel_id=1, source_target_pairs={{0,1},{1,2},{2,3},{3,0},{4,5},{5,6},{6,7},{7,4},{8,9},{9,10},{10,1... | collective-permute-start | bytes 196616 | tf_op jit(solution)/shard_map/ppermute | solution.py:12
  26.6 7.5 %collective-permute-start.1 = (bf16[32,1024]{1,0:T(8,128)(2,1)S(1)}, bf16[32,1024]{1,0:T(8,128)(2,1)S(1)}, u32[]{:S(2)}, u32[]{:S(2)}) collective-permute-start(bf16[32,1024]{1,0:T(8,128)(2,1)S(1)} %collective-permute-done), channel_id=1, source_target_pairs={{0,1},{1,2},{2,3},{3,0},{4,5},{5,6},{6,7},{7,4},{8,9},{9,10},{10,1... | collective-permute-start | bytes 196616 | tf_op jit(solution)/shard_map/ppermute | solution.py:12
  34.1 7.6 %collective-permute-start.2 = (bf16[32,1024]{1,0:T(8,128)(2,1)S(1)}, bf16[32,1024]{1,0:T(8,128)(2,1)S(1)}, u32[]{:S(2)}, u32[]{:S(2)}) collective-permute-start(bf16[32,1024]{1,0:T(8,128)(2,1)S(1)} %collective-permute-done.1), channel_id=1, source_target_pairs={{0,1},{1,2},{2,3},{3,0},{4,5},{5,6},{6,7},{7,4},{8,9},{9,10},{10,1... | collective-permute-start | bytes 196616 | tf_op jit(solution)/shard_map/ppermute | solution.py:12
  44.3 0.7 copy-start.2
Sparse Core Ops, SparseCore 0:
  8.9 35.3 all-gather.2
